TPU v7x, 32 devices: a whole 2x2x4 slice. The times are simulated.
32 devices in a mesh: ctx: 4 (over y, core), head: 4 (over z), wide: 2 (over x).
Axes of the slice: x: 2, y: 2, z: 4, core: 2. Of those that a mesh axis runs over, the one named last changes fastest.
Arguments:
- query_rows: bfloat16 [2, 1024, 1024], P('wide', 'ctx', 'head'), may hold values from -105 to 105
- key_rows: bfloat16 [2, 1024, 1024], P('wide', 'ctx', 'head'), may hold values from -4.5 to 4.5
- value_rows: bfloat16 [2, 1024, 1024], P('wide', 'ctx', 'head'), may hold values from -6 to 6
- grad_out: bfloat16 [2, 1024, 1024], P('wide', 'ctx', 'head'), may hold values from -6 to 6
- segment: int32 [2, 1024], P('wide', 'ctx'), may hold values from 0 to 7, never falling along the last dimension, each value on 1 to 256 neighbouring positions
- frames: bfloat16 [2, 1024, 4096], P(None, 'ctx', 'wide'), may hold values from -6 to 6
Outputs:
- grad_query: bfloat16 [2, 1024, 1024], P('wide', 'ctx', 'head')
- grad_key: bfloat16 [2, 1024, 1024], P('wide', 'ctx', 'head')
- grad_value: bfloat16 [2, 1024, 1024], P('wide', 'ctx', 'head')
- grad_wq: float32 [2, 2048, 1024], P('wide', 'ctx', 'head')
Inputs may be any that keep to these rules, and one draw needn't show every extreme that they name: Ids never fall along a recording; each segment spans 1 to 256 frames and one spans exactly 256.
All inputs are finite; a program needn't handle non-finite values.
Results may differ from a plain program's by a relative error of at most 0.01.
Values may be sent and summed in bfloat16 or wider, within the bound.
No kernel may reach another device: no remote copies, remote signals or barrier semaphores. Data moves between devices by JAX's collectives and lax.ppermute only.
A program may use at most 64 MiB of HBM per device.

v0:
```python
import jax
import jax.numpy as jnp
from jax import lax
from jax.sharding import PartitionSpec as P

HD = 128


def shifted(value, axis, steps):
    count = lax.axis_size(axis)
    initial, last = (max(0, -steps), min(count, count - steps))
    return lax.ppermute(value, axis, [(source, source + steps) for source in range(initial, last)])


def head_scores(left_heads, right_heads):
    return jnp.einsum("ihd,jhd->hij", left_heads, right_heads, preferred_element_type=jnp.float32)


def shards(query_rows, key_rows, value_rows, grad_out, segment, frames):
    length = query_rows.shape[1]
    columns = query_rows.shape[2]
    head_count = columns // HD
    factor = HD ** (-0.5)
    ctx_index = lax.axis_index("ctx")
    ctx_count = lax.axis_size("ctx")
    query_heads = query_rows.reshape(length, head_count, HD)
    key_heads = key_rows.reshape(length, head_count, HD)
    value_heads = value_rows.reshape(length, head_count, HD)
    grad_heads = grad_out.reshape(length, head_count, HD)
    own_segment = segment[0]
    prior_keys, prior_values, prior_segment = shifted((key_rows, value_rows, segment), "ctx", 1)
    prior_key_heads = prior_keys.reshape(length, head_count, HD)
    prior_value_heads = prior_values.reshape(length, head_count, HD)
    places = jnp.arange(length, dtype=jnp.int32)
    own_mask = (own_segment[:, None] == own_segment[None, :]) & (places[None, :] <= places[:, None])
    prior_mask = (own_segment[:, None] == prior_segment[0][None, :]) & (ctx_index > 0)
    own_scores = head_scores(query_heads, key_heads) * factor
    prior_scores = head_scores(query_heads, prior_key_heads) * factor
    row_max = jnp.maximum(
        jnp.max(jnp.where(own_mask, own_scores, -jnp.inf), axis=2, keepdims=True),
        jnp.max(jnp.where(prior_mask, prior_scores, -jnp.inf), axis=2, keepdims=True),
    )
    row_total = jnp.sum(
        jnp.where(own_mask, jnp.exp(own_scores - row_max), 0.0), axis=2, keepdims=True
    ) + jnp.sum(jnp.where(prior_mask, jnp.exp(prior_scores - row_max), 0.0), axis=2, keepdims=True)
    log_total = row_max + jnp.log(row_total)
    own_prob = jnp.where(own_mask, jnp.exp(own_scores - log_total), 0.0)
    prior_prob = jnp.where(prior_mask, jnp.exp(prior_scores - log_total), 0.0)
    own_grad_prob = head_scores(grad_heads, value_heads)
    prior_grad_prob = head_scores(grad_heads, prior_value_heads)
    row_delta = jnp.sum(own_prob * own_grad_prob, axis=2, keepdims=True) + jnp.sum(
        prior_prob * prior_grad_prob, axis=2, keepdims=True
    )
    own_grad_score = (own_prob * (own_grad_prob - row_delta)).astype(jnp.bfloat16)
    prior_grad_score = (prior_prob * (prior_grad_prob - row_delta)).astype(jnp.bfloat16)
    own_prob_low = own_prob.astype(jnp.bfloat16)
    grad_query_heads = (
        jnp.einsum("hij,jhd->ihd", own_grad_score, key_heads, preferred_element_type=jnp.float32)
        + jnp.einsum(
            "hij,jhd->ihd", prior_grad_score, prior_key_heads, preferred_element_type=jnp.float32
        )
    ) * factor
    grad_query = grad_query_heads.astype(jnp.bfloat16).reshape(1, length, columns)
    own_key_grad = jnp.einsum(
        "hij,ihd->jhd", own_grad_score, query_heads, preferred_element_type=jnp.float32
    )
    own_value_grad = jnp.einsum(
        "hij,ihd->jhd", own_prob_low, grad_heads, preferred_element_type=jnp.float32
    )
    prior_key_grad = jnp.einsum(
        "hij,ihd->jhd", prior_grad_score, query_heads, preferred_element_type=jnp.float32
    )
    prior_value_grad = jnp.einsum(
        "hij,ihd->jhd",
        prior_prob.astype(jnp.bfloat16),
        grad_heads,
        preferred_element_type=jnp.float32,
    )
    later_key_grad, later_value_grad = shifted((prior_key_grad, prior_value_grad), "ctx", -1)
    grad_key = (
        ((own_key_grad + later_key_grad) * factor).astype(jnp.bfloat16).reshape(1, length, columns)
    )
    grad_value = (
        (own_value_grad + later_value_grad).astype(jnp.bfloat16).reshape(1, length, columns)
    )
    width = frames.shape[2]
    row_block = width // ctx_count
    panel_sum = jnp.einsum(
        "rtd,rtc->dc",
        frames,
        lax.all_gather(grad_query, "wide", axis=0, tiled=True),
        preferred_element_type=jnp.float32,
    )
    grad_wq = lax.psum_scatter(panel_sum, "ctx", scatter_dimension=0, tiled=True).reshape(
        1, row_block, columns
    )
    return (grad_query, grad_key, grad_value, grad_wq)


def solution(mesh):
    return jax.shard_map(
        shards,
        mesh=mesh,
        in_specs=(
            P("wide", "ctx", "head"),
            P("wide", "ctx", "head"),
            P("wide", "ctx", "head"),
            P("wide", "ctx", "head"),
            P("wide", "ctx"),
            P(None, "ctx", "wide"),
        ),
        out_specs=(
            P("wide", "ctx", "head"),
            P("wide", "ctx", "head"),
            P("wide", "ctx", "head"),
            P("wide", "ctx", "head"),
        ),
        check_vma=False,
    )
```

profile of v0, /device:TPU:0, one launch (start us, length us, event | category | flops | bytes accessed | tf_op | source)
XLA Modules:
  0.0 79.4 jit_solution(1340995519553160902)
XLA Ops:
  7.2 0.0 copy-start
  7.2 0.0 copy-start.9
  7.2 0.0 reduce-scatter.2.cloned.1.call-start
  7.2 2.5 %collective-permute-start = (s32[1,256]{1,0:T(1,128)}, s32[1,256]{1,0:T(1,128)S(1)}, u32[]{:S(2)}, u32[]{:S(2)}) collective-permute-start(s32[1,256]{1,0:T(1,128)} %param.10), channel_id=1, source_target_pairs={{0,8},{8,16},{16,24},{1,9},{9,17},{17,25},{2,10},{10,18},{18,26},{... | collective-permute-start | bytes 3080 | tf_op jit(solution)/shard_map/ppermute | solution.py:12
  9.8 1.7 %copy.64 = bf16[1,256,256]{1,2,0:T(8,128)(2,1)} copy(bf16[1,256,256]{2,1,0:T(8,128)(2,1)} %param.8) | data formatting | bytes 262144 | tf_op args[2]
  11.4 5.2 %collective-permute-start.2 = (bf16[1,256,256]{1,2,0:T(8,128)(2,1)}, bf16[1,256,256]{1,2,0:T(8,128)(2,1)}, u32[]{:S(2)}, u32[]{:S(2)}) collective-permute-start(bf16[1,256,256]{1,2,0:T(8,128)(2,1)} %copy.64), channel_id=1, source_target_pairs={{0,8},{8,16},{16,24},{1,9},{9,17},{17,25},{2,10},{10,18},{18,26},{... | collective-permute-start | bytes 393224 | tf_op jit(solution)/shard_map/ppermute | solution.py:12
  16.6 1.0 %copy.93 = bf16[1,256,256]{1,2,0:T(8,128)(2,1)S(1)} copy(bf16[1,256,256]{2,1,0:T(8,128)(2,1)} %param.7) | data formatting | bytes 262144 | tf_op jit(solution)/shard_map/reshape | solution.py:27
  17.6 0.0 copy-start.5
  17.6 1.3 %collective-permute-start.1 = (bf16[1,256,256]{1,2,0:T(8,128)(2,1)S(1)}, bf16[1,256,256]{1,2,0:T(8,128)(2,1)S(1)}, u32[]{:S(2)}, u32[]{:S(2)}) collective-permute-start(bf16[1,256,256]{1,2,0:T(8,128)(2,1)S(1)} %copy.93), channel_id=1, source_target_pairs={{0,8},{8,16},{16,24},{1,9},{9,17},{17,25},{2,10},{10,18},{18,26},{... | collective-permute-start | bytes 393224 | tf_op jit(solution)/shard_map/ppermute | solution.py:12
  18.9 0.9 %reshape.69 = bf16[256,2,128]{2,1,0:T(2,128)(2,1)S(1)} reshape(bf16[1,256,256]{2,1,0:T(8,128)(2,1)} %param.8) | data formatting | bytes 262144 | tf_op jit(solution)/shard_map/reshape | solution.py:28
  19.9 0.9 %reshape.68 = bf16[256,2,128]{2,1,0:T(2,128)(2,1)S(1)} reshape(bf16[1,256,256]{2,1,0:T(8,128)(2,1)} %param.9) | data formatting | bytes 262144 | tf_op jit(solution)/shard_map/reshape | solution.py:29
  20.8 1.0 %fusion.18 = f32[2,256,256]{1,2,0:T(8,128)} fusion(bf16[256,2,128]{2,1,0:T(2,128)(2,1)S(1)} %reshape.69, bf16[256,2,128]{2,1,0:T(2,128)(2,1)S(1)} %reshape.68), kind=kOutput, calls=%fused_computation.36 | convolution fusion | flops 33554432 | bytes 786432 | tf_op jit(solution)/shard_map/ihd,jhd->hij/dot_general | solution.py:16
  21.8 0.9 %reshape.65 = bf16[256,2,128]{2,1,0:T(2,128)(2,1)S(1)} reshape(bf16[1,256,256]{2,1,0:T(8,128)(2,1)} %param.6) | data formatting | bytes 262144 | tf_op jit(solution)/shard_map/reshape | solution.py:26
  22.8 0.0 copy-start.1
  22.8 0.0 collective-permute-done
  22.8 0.0 copy-done.9
  22.8 0.1 compare_and_fusion
  23.0 0.3 select_reduce_fusion.3
  23.3 0.0 collective-permute-done.1
  23.3 0.0 copy-start.7
  23.3 0.0 copy-done.5
  23.3 0.6 copy-done.7
  23.9 1.2 %select_reduce_fusion.2 = (f32[2,256]{1,0:T(2,128)S(1)}, f32[2,256,256]{1,2,0:T(8,128)S(1)}) fusion(pred[256,256]{0,1:T(8,128)(4,1)S(1)} %get-tuple-element.22, bf16[256,2,128]{0,2,1:T(8,128)(2,1)} %bitcast.50, bf16[256,2,128]{2,1,0:T(2,128)(2,1)S(1)} %reshape.65), kind=kOutput, calls=%fused_computation.23 | convolution fusion | flops 33947136 | bytes 854016 | tf_op jit(solution)/shard_map/ihd,jhd->hij/dot_general | solution.py:16
  25.1 0.2 select_reduce_fusion
  25.4 0.0 collective-permute-done.2
  25.4 0.0 copy-done.1
  25.4 0.0 copy-start.6
  25.4 1.4 %multiply_reduce_fusion = (f32[2,256]{1,0:T(2,128)S(1)}, f32[2,256]{1,0:T(2,128)S(1)}, f32[2,256,256]{1,2,0:T(8,128)S(1)}) fusion(f32[2,256,256]{1,2,0:T(8,128)S(1)} %get-tuple-element.27, f32[2,256]{1,0:T(2,128)S(1)} %log_add_fusion, pred[256,256]{0,1:T(8,128)(4,1)S(1)} %get-tuple-element.22, f32[2,256,256]{1,2,0:T(8,128)S(1)} %copy-done.1, ...), kind=kOutput, calls=%fused_computation.17 | convolution fusion | flops 34601984 | bytes 2496512 | tf_op jit(solution)/shard_map/ihd,jhd->hij/dot_general | solution.py:16
  26.8 0.0 copy-start.8
  26.8 0.3 multiply_convert_fusion
  27.1 0.0 copy-start.2
  27.1 0.0 copy-start.4
  27.1 0.7 copy-done.2
  27.8 0.0 copy-done.6
  27.8 0.2 fusion.31
  28.0 0.0 copy-done.4
  28.0 0.0 copy-done.8
  28.0 0.8 %fusion.6 = bf16[2,256,128]{1,2,0:T(8,128)(2,1)} fusion(f32[2,256,128]{1,2,0:T(8,128)S(1)} %fusion.31, bf16[256,2,128]{0,2,1:T(8,128)(2,1)S(1)} %bitcast.51, bf16[2,256,256]{1,2,0:T(8,128)(2,1)S(1)} %get-tuple-element.20), kind=kOutput, calls=%fused_computation.14 | convolution fusion | flops 33751040 | bytes 786432 | tf_op jit(solution)/shard_map/hij,jhd->ihd/dot_general | solution.py:59
  28.9 1.7 %copy.80 = bf16[1,256,256]{2,1,0:T(8,128)(2,1)} copy(bf16[1,256,256]{1,2,0:T(8,128)(2,1)} %bitcast.49) | data formatting | bytes 262144
  30.5 6.3 %all_gather.3 = bf16[2,256,256]{2,1,0:T(8,128)(2,1)S(1)} all-gather(bf16[1,256,256]{2,1,0:T(8,128)(2,1)} %copy.80), channel_id=1, replica_groups=mesh['ctx'=4,'head'=4,'wide'=2] {'wide'}, dimensions={0}, use_global_device_ids=true | all-gather | bytes 393216 | tf_op jit(solution)/shard_map/all_gather | solution.py:91
  36.8 0.0 copy-done
  36.8 2.1 %convolution_bitcast_fusion = f32[2048,256]{0,1:T(8,128)} fusion(bf16[2,256,256]{2,1,0:T(8,128)(2,1)S(1)} %all_gather.3, bf16[2,256,2048]{2,1,0:T(8,128)(2,1)S(1)} %copy-done), kind=kOutput, calls=%fused_computation | convolution fusion | flops 536870912 | bytes 4456448 | tf_op jit(solution)/shard_map/rtd,rtc->dc/dot_general | solution.py:88
  38.9 0.0 reduce-scatter.2.cloned.1.call-update
  38.9 0.2 convolution_bitcast_fusion.1
  39.1 0.0 copy-start.3
  39.2 1.4 %collective-permute-start.4 = (f32[256,2,128]{0,2,1:T(8,128)S(1)}, f32[256,2,128]{0,2,1:T(8,128)S(1)}, u32[]{:S(2)}, u32[]{:S(2)}) collective-permute-start(f32[256,2,128]{0,2,1:T(8,128)S(1)} %convolution_bitcast_fusion.1), channel_id=1, source_target_pairs={{8,0},{16,8},{24,16},{9,1},{17,9},{25,17},{10,2},{18,10},{26,18},{... | collective-permute-start | bytes 786440 | tf_op jit(solution)/shard_map/ppermute | solution.py:12
  40.6 1.9 %convolution_bitcast_fusion.3 = f32[256,2,128]{0,2,1:T(8,128)} fusion(bf16[2,256,256]{1,2,0:T(8,128)(2,1)} %copy-done.4, bf16[256,2,128]{2,1,0:T(2,128)(2,1)S(1)} %reshape.65), kind=kOutput, calls=%fused_computation.8 | convolution fusion | flops 33554432 | bytes 655360 | tf_op jit(solution)/shard_map/hij,ihd->jhd/dot_general | solution.py:70
  42.5 1.3 %collective-permute-start.3 = (f32[256,2,128]{0,2,1:T(8,128)}, f32[256,2,128]{0,2,1:T(8,128)}, u32[]{:S(2)}, u32[]{:S(2)}) collective-permute-start(f32[256,2,128]{0,2,1:T(8,128)} %convolution_bitcast_fusion.3), channel_id=1, source_target_pairs={{8,0},{16,8},{24,16},{9,1},{17,9},{25,17},{10,2},{18,10},{26,18},{... | collective-permute-start | bytes 786440 | tf_op jit(solution)/shard_map/ppermute | solution.py:12
  43.7 0.0 collective-permute-done.4
  43.7 0.2 fusion.5
  44.0 0.8 copy.82
  44.8 2.3 %collective-permute-done.3 = f32[256,2,128]{0,2,1:T(8,128)} collective-permute-done((f32[256,2,128]{0,2,1:T(8,128)}, f32[256,2,128]{0,2,1:T(8,128)}, u32[]{:S(2)}, u32[]{:S(2)}) %collective-permute-start.3) | collective-permute-done | bytes 262176 | tf_op jit(solution)/shard_map/ppermute | solution.py:12
  47.1 0.0 copy-done.3
  47.1 1.2 %fusion.4 = bf16[256,2,128]{0,2,1:T(8,128)(2,1)S(1)} fusion(f32[256,2,128]{0,2,1:T(8,128)} %collective-permute-done.3, bf16[2,256,256]{1,2,0:T(8,128)(2,1)S(1)} %copy-done.3, bf16[256,2,128]{2,1,0:T(2,128)(2,1)S(1)} %reshape.65), kind=kOutput, calls=%fused_computation.12 | convolution fusion | flops 33751040 | bytes 786432 | tf_op jit(solution)/shard_map/hij,ihd->jhd/dot_general | solution.py:64
  48.3 0.8 copy.81
  49.1 21.4 %reduce-scatter.2.cloned.1.call-done = f32[512,256]{0,1:T(8,128)} async-done(((f32[2048,256]{0,1:T(8,128)}), f32[512,256]{0,1:T(8,128)}) %reduce-scatter.2.cloned.1.call-update) | async-done | bytes 524304 | tf_op jit(solution)/shard_map/reduce_scatter | solution.py:94
  70.5 2.0 %copy.83 = f32[1,512,256]{2,1,0:T(8,128)} copy(f32[1,512,256]{1,2,0:T(8,128)} %bitcast.47) | data formatting | bytes 1048576
  (3 shorter events, 0.0 us)
Async XLA Ops:
  7.2 29.6 %copy-start = (bf16[2,256,2048]{2,1,0:T(8,128)(2,1)S(1)}, bf16[2,256,2048]{2,1,0:T(8,128)(2,1)}, u32[]{:S(2)}) copy-start(bf16[2,256,2048]{2,1,0:T(8,128)(2,1)} %param.11) | copy-start | bytes 6291460
  7.2 15.6 %copy-start.9 = (s32[1,256]{1,0:T(1,128)S(1)}, s32[1,256]{1,0:T(1,128)}, u32[]{:S(2)}) copy-start(s32[1,256]{1,0:T(1,128)} %param.10) | copy-start | bytes 3076
  7.2 63.3 %reduce-scatter.2.cloned.1.call-start = ((), (), s32[]{:S(2)}) async-start(), calls=%async_computation.1 | async-start | bytes 2621440 | tf_op jit(solution)/shard_map/reduce_scatter | solution.py:94
  7.2 15.6 %collective-permute-start = (s32[1,256]{1,0:T(1,128)}, s32[1,256]{1,0:T(1,128)S(1)}, u32[]{:S(2)}, u32[]{:S(2)}) collective-permute-start(s32[1,256]{1,0:T(1,128)} %param.10), channel_id=1, source_target_pairs={{0,8},{8,16},{16,24},{1,9},{9,17},{17,25},{2,10},{10,18},{18,26},{... | collective-permute-start | bytes 3080 | tf_op jit(solution)/shard_map/ppermute | solution.py:12
  11.4 13.9 %collective-permute-start.2 = (bf16[1,256,256]{1,2,0:T(8,128)(2,1)}, bf16[1,256,256]{1,2,0:T(8,128)(2,1)}, u32[]{:S(2)}, u32[]{:S(2)}) collective-permute-start(bf16[1,256,256]{1,2,0:T(8,128)(2,1)} %copy.64), channel_id=1, source_target_pairs={{0,8},{8,16},{16,24},{1,9},{9,17},{17,25},{2,10},{10,18},{18,26},{... | collective-permute-start | bytes 393224 | tf_op jit(solution)/shard_map/ppermute | solution.py:12
  17.6 5.7 %copy-start.5 = (bf16[1,256,256]{1,2,0:T(8,128)(2,1)}, bf16[1,256,256]{1,2,0:T(8,128)(2,1)S(1)}, u32[]{:S(2)}) copy-start(bf16[1,256,256]{1,2,0:T(8,128)(2,1)S(1)} %copy.93) | copy-start | bytes 393220
  17.6 5.6 %collective-permute-start.1 = (bf16[1,256,256]{1,2,0:T(8,128)(2,1)S(1)}, bf16[1,256,256]{1,2,0:T(8,128)(2,1)S(1)}, u32[]{:S(2)}, u32[]{:S(2)}) collective-permute-start(bf16[1,256,256]{1,2,0:T(8,128)(2,1)S(1)} %copy.93), channel_id=1, source_target_pairs={{0,8},{8,16},{16,24},{1,9},{9,17},{17,25},{2,10},{10,18},{18,26},{... | collective-permute-start | bytes 393224 | tf_op jit(solution)/shard_map/ppermute | solution.py:12
  22.8 2.6 %copy-start.1 = (f32[2,256,256]{1,2,0:T(8,128)S(1)}, f32[2,256,256]{1,2,0:T(8,128)}, u32[]{:S(2)}) copy-start(f32[2,256,256]{1,2,0:T(8,128)} %fusion.18) | copy-start | bytes 1572868
  23.3 0.7 copy-start.7
  25.4 2.4 %copy-start.6 = (bf16[1,256,256]{1,2,0:T(8,128)(2,1)S(1)}, bf16[1,256,256]{1,2,0:T(8,128)(2,1)}, u32[]{:S(2)}) copy-start(bf16[1,256,256]{1,2,0:T(8,128)(2,1)} %copy-done.5) | copy-start | bytes 393220
  26.8 1.2 %copy-start.8 = (bf16[1,256,256]{1,2,0:T(8,128)(2,1)S(1)}, bf16[1,256,256]{1,2,0:T(8,128)(2,1)}, u32[]{:S(2)}) copy-start(bf16[1,256,256]{1,2,0:T(8,128)(2,1)} %copy-done.7) | copy-start | bytes 393220
  27.1 0.7 copy-start.2
  27.1 0.9 %copy-start.4 = (bf16[2,256,256]{1,2,0:T(8,128)(2,1)}, bf16[2,256,256]{1,2,0:T(8,128)(2,1)S(1)}, u32[]{:S(2)}) copy-start(bf16[2,256,256]{1,2,0:T(8,128)(2,1)S(1)} %get-tuple-element.20) | copy-start | bytes 786436
  39.1 8.0 %copy-start.3 = (bf16[2,256,256]{1,2,0:T(8,128)(2,1)S(1)}, bf16[2,256,256]{1,2,0:T(8,128)(2,1)}, u32[]{:S(2)}) copy-start(bf16[2,256,256]{1,2,0:T(8,128)(2,1)} %copy-done.2) | copy-start | bytes 786436
  39.2 4.6 %collective-permute-start.4 = (f32[256,2,128]{0,2,1:T(8,128)S(1)}, f32[256,2,128]{0,2,1:T(8,128)S(1)}, u32[]{:S(2)}, u32[]{:S(2)}) collective-permute-start(f32[256,2,128]{0,2,1:T(8,128)S(1)} %convolution_bitcast_fusion.1), channel_id=1, source_target_pairs={{8,0},{16,8},{24,16},{9,1},{17,9},{25,17},{10,2},{18,10},{26,18},{... | collective-permute-start | bytes 786440 | tf_op jit(solution)/shard_map/ppermute | solution.py:12
  42.5 4.6 %collective-permute-start.3 = (f32[256,2,128]{0,2,1:T(8,128)}, f32[256,2,128]{0,2,1:T(8,128)}, u32[]{:S(2)}, u32[]{:S(2)}) collective-permute-start(f32[256,2,128]{0,2,1:T(8,128)} %convolution_bitcast_fusion.3), channel_id=1, source_target_pairs={{8,0},{16,8},{24,16},{9,1},{17,9},{25,17},{10,2},{18,10},{26,18},{... | collective-permute-start | bytes 786440 | tf_op jit(solution)/shard_map/ppermute | solution.py:12
Sparse Core Ops, SparseCore 0:
  39.0 31.4 reduce-scatter.1
where the time goes:
time: 79.9 us; the launch traced here: 79.4 us
  waiting for transfers between devices  23.8 us (30%)
  between operations  14.3 us (18%)
  local copies, waits for them, and re-layouts  12.1 us (15%)
  starting transfers between devices  11.7 us (15%)
  matrix products  10.5 us (13%)
  blocking collectives  6.28 us (8%)
    reduce_scatter x1, waiting for transfers between devices, shards(): lax.psum_scatter(panel_sum, 'ctx', scatter_dimension=0, tiled=True)  21.4 us
    ppermute x5, starting transfers between devices, shifted(): lax.ppermute(value, axis, [(source, source + steps) for source in range(i...  11.7 us
    unnamed x25, local copies, waits for them, and re-layouts  8.25 us
    all_gather x1, blocking collectives, shards(): lax.all_gather(grad_query, 'wide', axis=0, tiled=True)  6.28 us
    dot_general x4, matrix products, head_scores(): jnp.einsum('ihd,jhd->hij', left_heads, right_heads, preferred_element_typ...  3.87 us
    ppermute x5, waiting for transfers between devices, shifted(): lax.ppermute(value, axis, [(source, source + steps) for source in range(i...  2.34 us
    dot_general x1, matrix products, shards(): jnp.einsum('rtd,rtc->dc', frames, lax.all_gather(grad_query, 'wide', axis...  2.06 us
    dot_general x1, matrix products, shards(): jnp.einsum('hij,ihd->jhd', prior_grad_score, query_heads, preferred_eleme...  1.87 us
  transfers between devices with their start and end apart: 6, of which 2 were waited for; matrix products, arithmetic and copies ran while one was open for 17% of the time, Pallas kernels for 0%

commit v1 on v0

--- a/solution.py
+++ b/solution.py
@@ -85,12 +85,20 @@
     )
     width = frames.shape[2]
     row_block = width // ctx_count
-    panel_sum = jnp.einsum(
-        "rtd,rtc->dc",
-        frames,
-        lax.all_gather(grad_query, "wide", axis=0, tiled=True),
-        preferred_element_type=jnp.float32,
-    )
+    size, here, rows = (lax.axis_size("wide"), lax.axis_index("wide"), grad_query.shape[0])
+    upward = [(i, (i + 1) % size) for i in range(size)]
+    carried, so_far = (grad_query, None)
+    for turn in range(size):
+        following = lax.ppermute(carried, "wide", upward) if turn < size - 1 else None
+        take_in = jnp.einsum(
+            "rtd,rtc->dc",
+            lax.dynamic_slice_in_dim(frames, (here - turn) % size * rows, carried.shape[0], axis=0),
+            carried,
+            preferred_element_type=jnp.float32,
+        )
+        so_far = take_in if so_far is None else so_far + take_in
+        carried = following
+    panel_sum = so_far
     grad_wq = lax.psum_scatter(panel_sum, "ctx", scatter_dimension=0, tiled=True).reshape(
         1, row_block, columns
     )

time: 79.9 us -> 75.1 us (0.940)
  blocking collectives: 6.28 us -> 0 us
  local copies, waits for them, and re-layouts: 12.1 us -> 8.72 us
  matrix products: 10.5 us -> 13.5 us
  starting transfers between devices: 11.7 us -> 13.7 us
    all_gather x1 -> x0, blocking collectives: 6.28 us -> none  [shards(): lax.all_gather(grad_query, 'wide', axis=0, tiled=True)]
    unnamed x25 -> x18, local copies, waits for them, and re-layouts: 8.25 us -> 4.9 us
    ppermute x5, waiting for transfers between devices: 2.34 us -> 0.01 us  [shifted(): lax.ppermute(value, axis, [(source, source + steps) for source in range(i...]
    ppermute x0 -> x1, waiting for transfers between devices: none -> 2.25 us  [shards(): lax.ppermute(carried, 'wide', upward)]
    ppermute x0 -> x1, starting transfers between devices: none -> 1.5 us  [shards(): lax.ppermute(carried, 'wide', upward)]
    dot_general x1 -> x2, matrix products: 2.06 us -> 3.28 us  [shards(): jnp.einsum('rtd,rtc->dc', lax.dynamic_slice_in_dim(frames, (here - turn)...]
    dot_general x1, matrix products: 0.85 us -> 1.75 us  [shards(): jnp.einsum('hij,jhd->ihd', prior_grad_score, prior_key_heads, preferred_e...]
  transfers between devices with their start and end apart: 6 -> 7, of which waited for: 2 -> 2; matrix products, arithmetic and copies ran while one was open for 17% -> 23% of each run, Pallas kernels for 0% -> 0%
where the time goes in v1:
time: 75.1 us; the launch traced here: 74.6 us
  waiting for transfers between devices  23.7 us (32%)
  between operations  14.3 us (19%)
  starting transfers between devices  13.7 us (18%)
  matrix products  13.5 us (18%)
  local copies, waits for them, and re-layouts  8.72 us (12%)
    reduce_scatter x1, waiting for transfers between devices, shards(): lax.psum_scatter(panel_sum, 'ctx', scatter_dimension=0, tiled=True)  21.4 us
    ppermute x5, starting transfers between devices, shifted(): lax.ppermute(value, axis, [(source, source + steps) for source in range(i...  12.2 us
    unnamed x18, local copies, waits for them, and re-layouts  4.9 us
    dot_general x4, matrix products, head_scores(): jnp.einsum('ihd,jhd->hij', left_heads, right_heads, preferred_element_typ...  3.89 us
    dot_general x2, matrix products, shards(): jnp.einsum('rtd,rtc->dc', lax.dynamic_slice_in_dim(frames, (here - turn)...  3.28 us
    ppermute x1, waiting for transfers between devices, shards(): lax.ppermute(carried, 'wide', upward)  2.25 us
    dot_general x1, matrix products, shards(): jnp.einsum('hij,ihd->jhd', prior_grad_score, query_heads, preferred_eleme...  1.89 us
    dot_general x1, matrix products, shards(): jnp.einsum('hij,jhd->ihd', prior_grad_score, prior_key_heads, preferred_e...  1.75 us
  transfers between devices with their start and end apart: 7, of which 2 were waited for; matrix products, arithmetic and copies ran while one was open for 23% of the time, Pallas kernels for 0%

profile of v1, /device:TPU:0, one launch (start us, length us, event | category | flops | bytes accessed | tf_op | source)
XLA Modules:
  0.0 74.6 jit_solution(3589378240633850144)
XLA Ops:
  7.2 0.0 copy-start
  7.2 0.0 copy-start.6
  7.2 0.0 reduce-scatter.2.cloned.1.call-start
  7.2 2.5 %collective-permute-start = (s32[1,256]{1,0:T(1,128)}, s32[1,256]{1,0:T(1,128)S(1)}, u32[]{:S(2)}, u32[]{:S(2)}) collective-permute-start(s32[1,256]{1,0:T(1,128)} %param.10), channel_id=1, source_target_pairs={{0,8},{8,16},{16,24},{1,9},{9,17},{17,25},{2,10},{10,18},{18,26},{... | collective-permute-start | bytes 3080 | tf_op jit(solution)/shard_map/ppermute | solution.py:12
  9.8 1.0 %copy.63 = bf16[1,256,256]{1,2,0:T(8,128)(2,1)S(1)} copy(bf16[1,256,256]{2,1,0:T(8,128)(2,1)} %param.7) | data formatting | bytes 262144 | tf_op jit(solution)/shard_map/reshape | solution.py:27
  10.8 0.0 copy-start.4
  10.8 5.2 %collective-permute-start.1 = (bf16[1,256,256]{1,2,0:T(8,128)(2,1)S(1)}, bf16[1,256,256]{1,2,0:T(8,128)(2,1)}, u32[]{:S(2)}, u32[]{:S(2)}) collective-permute-start(bf16[1,256,256]{1,2,0:T(8,128)(2,1)S(1)} %copy.63), channel_id=1, source_target_pairs={{0,8},{8,16},{16,24},{1,9},{9,17},{17,25},{2,10},{10,18},{18,26},{... | collective-permute-start | bytes 393224 | tf_op jit(solution)/shard_map/ppermute | solution.py:12
  16.0 1.7 %copy.38 = bf16[1,256,256]{1,2,0:T(8,128)(2,1)} copy(bf16[1,256,256]{2,1,0:T(8,128)(2,1)} %param.8) | data formatting | bytes 262144 | tf_op args[2]
  17.6 1.9 %collective-permute-start.2 = (bf16[1,256,256]{1,2,0:T(8,128)(2,1)}, bf16[1,256,256]{1,2,0:T(8,128)(2,1)}, u32[]{:S(2)}, u32[]{:S(2)}) collective-permute-start(bf16[1,256,256]{1,2,0:T(8,128)(2,1)} %copy.38), channel_id=1, source_target_pairs={{0,8},{8,16},{16,24},{1,9},{9,17},{17,25},{2,10},{10,18},{18,26},{... | collective-permute-start | bytes 393224 | tf_op jit(solution)/shard_map/ppermute | solution.py:12
  19.6 0.9 %reshape.82 = bf16[256,2,128]{2,1,0:T(2,128)(2,1)S(1)} reshape(bf16[1,256,256]{2,1,0:T(8,128)(2,1)} %param.8) | data formatting | bytes 262144 | tf_op jit(solution)/shard_map/reshape | solution.py:28
  20.5 0.9 %reshape.81 = bf16[256,2,128]{2,1,0:T(2,128)(2,1)S(1)} reshape(bf16[1,256,256]{2,1,0:T(8,128)(2,1)} %param.9) | data formatting | bytes 262144 | tf_op jit(solution)/shard_map/reshape | solution.py:29
  21.5 1.0 %fusion.24 = f32[2,256,256]{1,2,0:T(8,128)} fusion(bf16[256,2,128]{2,1,0:T(2,128)(2,1)S(1)} %reshape.82, bf16[256,2,128]{2,1,0:T(2,128)(2,1)S(1)} %reshape.81), kind=kOutput, calls=%fused_computation.42 | convolution fusion | flops 33554432 | bytes 786432 | tf_op jit(solution)/shard_map/ihd,jhd->hij/dot_general | solution.py:16
  22.5 0.9 %reshape.78 = bf16[256,2,128]{2,1,0:T(2,128)(2,1)S(1)} reshape(bf16[1,256,256]{2,1,0:T(8,128)(2,1)} %param.6) | data formatting | bytes 262144 | tf_op jit(solution)/shard_map/reshape | solution.py:26
  23.4 0.0 copy-start.1
  23.4 0.0 collective-permute-done
  23.5 0.0 copy-done.6
  23.5 0.1 compare_and_fusion
  23.6 0.3 select_reduce_fusion.3
  23.9 0.0 collective-permute-done.1
  23.9 0.0 copy-done.4
  23.9 1.2 %select_reduce_fusion.2 = (f32[2,256]{1,0:T(2,128)S(1)}, f32[2,256,256]{1,2,0:T(8,128)S(1)}) fusion(pred[256,256]{0,1:T(8,128)(4,1)S(1)} %get-tuple-element.18, bf16[256,2,128]{0,2,1:T(8,128)(2,1)} %bitcast.2, bf16[256,2,128]{2,1,0:T(2,128)(2,1)S(1)} %reshape.78), kind=kOutput, calls=%fused_computation.28 | convolution fusion | flops 33947136 | bytes 854016 | tf_op jit(solution)/shard_map/ihd,jhd->hij/dot_general | solution.py:16
  25.1 0.2 select_reduce_fusion
  25.4 0.0 collective-permute-done.2
  25.4 0.0 copy-done.1
  25.4 0.0 copy-start.5
  25.4 1.4 %multiply_reduce_fusion = (f32[2,256]{1,0:T(2,128)S(1)}, f32[2,256]{1,0:T(2,128)S(1)}, f32[2,256,256]{1,2,0:T(8,128)S(1)}) fusion(f32[2,256,256]{1,2,0:T(8,128)S(1)} %get-tuple-element.23, f32[2,256]{1,0:T(2,128)S(1)} %log_add_fusion, pred[256,256]{0,1:T(8,128)(4,1)S(1)} %get-tuple-element.18, f32[2,256,256]{1,2,0:T(8,128)S(1)} %copy-done.1, ...), kind=kOutput, calls=%fused_computation.22 | convolution fusion | flops 34601984 | bytes 2496512 | tf_op jit(solution)/shard_map/ihd,jhd->hij/dot_general | solution.py:16
  26.8 0.3 multiply_convert_fusion
  27.1 0.0 copy-start.2
  27.1 0.0 copy-start.3
  27.1 0.0 copy-done.5
  27.1 0.2 fusion.39
  27.3 1.8 %fusion.6 = bf16[2,256,128]{1,2,0:T(8,128)(2,1)} fusion(f32[2,256,128]{1,2,0:T(8,128)S(1)} %fusion.39, bf16[256,2,128]{0,2,1:T(8,128)(2,1)} %bitcast.2, bf16[2,256,256]{1,2,0:T(8,128)(2,1)S(1)} %get-tuple-element.16), kind=kOutput, calls=%fused_computation.14 | convolution fusion | flops 33751040 | bytes 786432 | tf_op jit(solution)/shard_map/hij,jhd->ihd/dot_general | solution.py:59
  29.1 1.5 %collective-permute-start.5 = (bf16[1,256,256]{1,2,0:T(8,128)(2,1)}, bf16[1,256,256]{1,2,0:T(8,128)(2,1)S(1)}, u32[]{:S(2)}, u32[]{:S(2)}) collective-permute-start(bf16[1,256,256]{1,2,0:T(8,128)(2,1)} %bitcast.5), channel_id=1, source_target_pairs={{0,1},{1,0},{2,3},{3,2},{4,5},{5,4},{6,7},{7,6},{8,9},{9,8},{10,11... | collective-permute-start | bytes 393224 | tf_op jit(solution)/shard_map/ppermute | solution.py:92
  30.6 0.0 copy-done.2
  30.6 0.0 copy-done.3
  30.6 0.0 copy-done
  30.6 1.4 %fusion.8 = f32[2048,256]{1,0:T(8,128)S(1)} fusion(bf16[256,256]{0,1:T(8,128)(2,1)} %bitcast.13, bf16[2,256,2048]{2,1,0:T(8,128)(2,1)S(1)} %copy-done, s32[]{:T(128)S(6)} %select_n.43), kind=kOutput, calls=%fused_computation.16 | convolution fusion | flops 268435456 | bytes 3276804 | tf_op jit(solution)/shard_map/rtd,rtc->dc/dot_general | solution.py:93
  32.0 2.3 %collective-permute-done.5 = bf16[1,256,256]{1,2,0:T(8,128)(2,1)S(1)} collective-permute-done((bf16[1,256,256]{1,2,0:T(8,128)(2,1)}, bf16[1,256,256]{1,2,0:T(8,128)(2,1)S(1)}, u32[]{:S(2)}, u32[]{:S(2)}) %collective-permute-start.5) | collective-permute-done | bytes 131104 | tf_op jit(solution)/shard_map/ppermute | solution.py:92
  34.3 1.9 %convolution_add_fusion = f32[2048,256]{1,0:T(8,128)} fusion(f32[2048,256]{1,0:T(8,128)S(1)} %fusion.8, bf16[2,256,2048]{2,1,0:T(8,128)(2,1)S(1)} %copy-done, s32[]{:T(128)S(6)} %select_n.45, bf16[1,256,256]{1,2,0:T(8,128)(2,1)S(1)} %collective-permute-done.5), kind=kOutput, calls=%fused_computation | convolution fusion | flops 268959744 | bytes 5373956 | tf_op jit(solution)/shard_map/rtd,rtc->dc/dot_general | solution.py:93
  36.1 0.0 reduce-scatter.2.cloned.1.call-update
  36.1 1.9 %convolution_bitcast_fusion.2 = f32[256,2,128]{0,2,1:T(8,128)} fusion(bf16[2,256,256]{1,2,0:T(8,128)(2,1)} %copy-done.3, bf16[256,2,128]{2,1,0:T(2,128)(2,1)S(1)} %reshape.78), kind=kOutput, calls=%fused_computation.8 | convolution fusion | flops 33554432 | bytes 655360 | tf_op jit(solution)/shard_map/hij,ihd->jhd/dot_general | solution.py:70
  38.0 1.3 %collective-permute-start.3 = (f32[256,2,128]{0,2,1:T(8,128)}, f32[256,2,128]{0,2,1:T(8,128)}, u32[]{:S(2)}, u32[]{:S(2)}) collective-permute-start(f32[256,2,128]{0,2,1:T(8,128)} %convolution_bitcast_fusion.2), channel_id=1, source_target_pairs={{8,0},{16,8},{24,16},{9,1},{17,9},{25,17},{10,2},{18,10},{26,18},{... | collective-permute-start | bytes 786440 | tf_op jit(solution)/shard_map/ppermute | solution.py:12
  39.3 1.0 %convolution_bitcast_fusion = f32[256,2,128]{0,2,1:T(8,128)} fusion(f32[2,256,256]{1,2,0:T(8,128)S(1)} %get-tuple-element.23, f32[2,256]{1,0:T(2,128)S(1)} %log_add_fusion, pred[256,256]{0,1:T(8,128)(4,1)S(1)} %get-tuple-element.18, bf16[256,2,128]{2,1,0:T(2,128)(2,1)S(1)} %reshape.81), kind=kOutput, calls=%fused_computation.5 | convolution fusion | flops 33947648 | bytes 985088 | tf_op jit(solution)/shard_map/hij,ihd->jhd/dot_general | solution.py:73
  40.3 1.3 %collective-permute-start.4 = (f32[256,2,128]{0,2,1:T(8,128)}, f32[256,2,128]{0,2,1:T(8,128)S(1)}, u32[]{:S(2)}, u32[]{:S(2)}) collective-permute-start(f32[256,2,128]{0,2,1:T(8,128)} %convolution_bitcast_fusion), channel_id=1, source_target_pairs={{8,0},{16,8},{24,16},{9,1},{17,9},{25,17},{10,2},{18,10},{26,18},{... | collective-permute-start | bytes 786440 | tf_op jit(solution)/shard_map/ppermute | solution.py:12
  41.6 1.7 %copy.52 = bf16[1,256,256]{2,1,0:T(8,128)(2,1)} copy(bf16[1,256,256]{1,2,0:T(8,128)(2,1)} %bitcast.5) | data formatting | bytes 262144
  43.3 0.0 collective-permute-done.3
  43.3 1.3 %fusion.4 = bf16[256,2,128]{0,2,1:T(8,128)(2,1)S(1)} fusion(f32[256,2,128]{0,2,1:T(8,128)} %collective-permute-done.3, bf16[2,256,256]{1,2,0:T(8,128)(2,1)} %copy-done.2, bf16[256,2,128]{2,1,0:T(2,128)(2,1)S(1)} %reshape.78), kind=kOutput, calls=%fused_computation.12 | convolution fusion | flops 33751040 | bytes 786432 | tf_op jit(solution)/shard_map/hij,ihd->jhd/dot_general | solution.py:64
  44.6 0.8 %copy.53 = bf16[1,256,256]{2,1,0:T(8,128)(2,1)} copy(bf16[1,256,256]{1,2,0:T(8,128)(2,1)S(1)} %bitcast.53) | data formatting | bytes 262144
  45.4 0.0 collective-permute-done.4
  45.4 0.2 fusion.5
  45.6 0.8 %copy.54 = bf16[1,256,256]{2,1,0:T(8,128)(2,1)} copy(bf16[1,256,256]{1,2,0:T(8,128)(2,1)S(1)} %bitcast.52) | data formatting | bytes 262144
  46.4 21.4 %reduce-scatter.2.cloned.1.call-done = f32[512,256]{1,0:T(8,128)} async-done(((f32[2048,256]{1,0:T(8,128)}), f32[512,256]{1,0:T(8,128)}) %reduce-scatter.2.cloned.1.call-update) | async-done | bytes 524304 | tf_op jit(solution)/shard_map/reduce_scatter | solution.py:102
  (3 shorter events, 0.0 us)
Async XLA Ops:
  7.2 23.4 %copy-start = (bf16[2,256,2048]{2,1,0:T(8,128)(2,1)S(1)}, bf16[2,256,2048]{2,1,0:T(8,128)(2,1)}, u32[]{:S(2)}) copy-start(bf16[2,256,2048]{2,1,0:T(8,128)(2,1)} %param.11) | copy-start | bytes 6291460
  7.2 16.3 %copy-start.6 = (s32[1,256]{1,0:T(1,128)S(1)}, s32[1,256]{1,0:T(1,128)}, u32[]{:S(2)}) copy-start(s32[1,256]{1,0:T(1,128)} %param.10) | copy-start | bytes 3076
  7.2 60.6 %reduce-scatter.2.cloned.1.call-start = ((), (), s32[]{:S(2)}) async-start(), calls=%async_computation.1 | async-start | bytes 2621440 | tf_op jit(solution)/shard_map/reduce_scatter | solution.py:102
  7.2 16.2 %collective-permute-start = (s32[1,256]{1,0:T(1,128)}, s32[1,256]{1,0:T(1,128)S(1)}, u32[]{:S(2)}, u32[]{:S(2)}) collective-permute-start(s32[1,256]{1,0:T(1,128)} %param.10), channel_id=1, source_target_pairs={{0,8},{8,16},{16,24},{1,9},{9,17},{17,25},{2,10},{10,18},{18,26},{... | collective-permute-start | bytes 3080 | tf_op jit(solution)/shard_map/ppermute | solution.py:12
  10.8 13.1 %copy-start.4 = (bf16[1,256,256]{1,2,0:T(8,128)(2,1)}, bf16[1,256,256]{1,2,0:T(8,128)(2,1)S(1)}, u32[]{:S(2)}) copy-start(bf16[1,256,256]{1,2,0:T(8,128)(2,1)S(1)} %copy.63) | copy-start | bytes 393220
  10.8 13.1 %collective-permute-start.1 = (bf16[1,256,256]{1,2,0:T(8,128)(2,1)S(1)}, bf16[1,256,256]{1,2,0:T(8,128)(2,1)}, u32[]{:S(2)}, u32[]{:S(2)}) collective-permute-start(bf16[1,256,256]{1,2,0:T(8,128)(2,1)S(1)} %copy.63), channel_id=1, source_target_pairs={{0,8},{8,16},{16,24},{1,9},{9,17},{17,25},{2,10},{10,18},{18,26},{... | collective-permute-start | bytes 393224 | tf_op jit(solution)/shard_map/ppermute | solution.py:12
  17.6 7.8 %collective-permute-start.2 = (bf16[1,256,256]{1,2,0:T(8,128)(2,1)}, bf16[1,256,256]{1,2,0:T(8,128)(2,1)}, u32[]{:S(2)}, u32[]{:S(2)}) collective-permute-start(bf16[1,256,256]{1,2,0:T(8,128)(2,1)} %copy.38), channel_id=1, source_target_pairs={{0,8},{8,16},{16,24},{1,9},{9,17},{17,25},{2,10},{10,18},{18,26},{... | collective-permute-start | bytes 393224 | tf_op jit(solution)/shard_map/ppermute | solution.py:12
  23.4 2.0 %copy-start.1 = (f32[2,256,256]{1,2,0:T(8,128)S(1)}, f32[2,256,256]{1,2,0:T(8,128)}, u32[]{:S(2)}) copy-start(f32[2,256,256]{1,2,0:T(8,128)} %fusion.24) | copy-start | bytes 1572868
  25.4 1.7 %copy-start.5 = (bf16[1,256,256]{1,2,0:T(8,128)(2,1)S(1)}, bf16[1,256,256]{1,2,0:T(8,128)(2,1)}, u32[]{:S(2)}) copy-start(bf16[1,256,256]{1,2,0:T(8,128)(2,1)} %copy-done.4) | copy-start | bytes 393220
  27.1 3.5 %copy-start.2 = (bf16[2,256,256]{1,2,0:T(8,128)(2,1)}, bf16[2,256,256]{1,2,0:T(8,128)(2,1)S(1)}, u32[]{:S(2)}) copy-start(bf16[2,256,256]{1,2,0:T(8,128)(2,1)S(1)} %get-tuple-element.17) | copy-start | bytes 786436
  27.1 3.5 %copy-start.3 = (bf16[2,256,256]{1,2,0:T(8,128)(2,1)}, bf16[2,256,256]{1,2,0:T(8,128)(2,1)S(1)}, u32[]{:S(2)}) copy-start(bf16[2,256,256]{1,2,0:T(8,128)(2,1)S(1)} %get-tuple-element.16) | copy-start | bytes 786436
  29.1 5.2 %collective-permute-start.5 = (bf16[1,256,256]{1,2,0:T(8,128)(2,1)}, bf16[1,256,256]{1,2,0:T(8,128)(2,1)S(1)}, u32[]{:S(2)}, u32[]{:S(2)}) collective-permute-start(bf16[1,256,256]{1,2,0:T(8,128)(2,1)} %bitcast.5), channel_id=1, source_target_pairs={{0,1},{1,0},{2,3},{3,2},{4,5},{5,4},{6,7},{7,6},{8,9},{9,8},{10,11... | collective-permute-start | bytes 393224 | tf_op jit(solution)/shard_map/ppermute | solution.py:92
  38.0 5.2 %collective-permute-start.3 = (f32[256,2,128]{0,2,1:T(8,128)}, f32[256,2,128]{0,2,1:T(8,128)}, u32[]{:S(2)}, u32[]{:S(2)}) collective-permute-start(f32[256,2,128]{0,2,1:T(8,128)} %convolution_bitcast_fusion.2), channel_id=1, source_target_pairs={{8,0},{16,8},{24,16},{9,1},{17,9},{25,17},{10,2},{18,10},{26,18},{... | collective-permute-start | bytes 786440 | tf_op jit(solution)/shard_map/ppermute | solution.py:12
  40.3 5.1 %collective-permute-start.4 = (f32[256,2,128]{0,2,1:T(8,128)}, f32[256,2,128]{0,2,1:T(8,128)S(1)}, u32[]{:S(2)}, u32[]{:S(2)}) collective-permute-start(f32[256,2,128]{0,2,1:T(8,128)} %convolution_bitcast_fusion), channel_id=1, source_target_pairs={{8,0},{16,8},{24,16},{9,1},{17,9},{25,17},{10,2},{18,10},{26,18},{... | collective-permute-start | bytes 786440 | tf_op jit(solution)/shard_map/ppermute | solution.py:12
Sparse Core Ops, SparseCore 0:
  36.3 31.4 reduce-scatter.1
